TPU v7x, 32 devices: a whole 2x2x4 slice. The times are simulated.
32 devices in a mesh: dp: 8 (over z, y), mp: 4 (over x, core).
Axes of the slice: x: 2, y: 2, z: 4, core: 2. Of those that a mesh axis runs over, the one named last changes fastest.
Arguments:
- tokens: bfloat16 [16384, 768], P('dp'), may hold values from -6 to 6
- lengths: int32 [8, 2], P('dp'), may hold values from 0 to 2048, as said below
- mix_gain: float32 [768], replicated, may hold values from 0.5 to 1.5
- mix_shift: float32 [768], replicated, may hold values from -4 to 4
- proj_in: bfloat16 [768, 3, 768], P(None, None, 'mp'), may hold values from -0.21875 to 0.21875
- bias_in: float32 [3, 768], P(None, 'mp'), may hold values from -4 to 4
- short_taps: float32 [3, 3, 768], P(None, None, 'mp'), may hold values from -6 to 6
- long_taps: bfloat16 [2048, 768], P('dp', 'mp'), may hold values from -0.75 to 0.75
- decay_rates: float32 [768], P('mp'), may hold values from 0.00024414062 to 0.05
- skip_gain: float32 [768], P('mp'), may hold values from -6 to 6
- proj_out: bfloat16 [768, 768], P('mp'), may hold values from -0.21875 to 0.21875
- bias_out: float32 [768], replicated, may hold values from -4 to 4
- mlp_gain: float32 [768], replicated, may hold values from 0.5 to 1.5
- mlp_shift: float32 [768], replicated, may hold values from -4 to 4
- proj_up: bfloat16 [768, 3072], P(None, 'mp'), may hold values from -0.21875 to 0.21875
- bias_up: float32 [3072], P('mp'), may hold values from -4 to 4
- proj_down: bfloat16 [3072, 768], P('mp'), may hold values from -0.109375 to 0.109375
- bias_down: float32 [768], replicated, may hold values from -4 to 4
- cotangent: bfloat16 [16384, 768], P('dp'), may hold values from -6 to 6
Outputs:
- output: bfloat16 [16384, 768], P('dp')
- input_grad: float32 [16384, 768], P('dp')
- grad_mix_gain: float32 [768], replicated
- grad_mix_shift: float32 [768], replicated
- grad_proj_in: float32 [768, 3, 768], P(None, None, 'mp')
- grad_bias_in: float32 [3, 768], P(None, 'mp')
- grad_short_taps: float32 [3, 3, 768], P(None, None, 'mp')
- grad_long_taps: float32 [2048, 768], P('dp', 'mp')
- grad_decay_rates: float32 [768], P('mp')
- grad_skip_gain: float32 [768], P('mp')
- grad_proj_out: float32 [768, 768], P('mp')
- grad_bias_out: float32 [768], replicated
- grad_mlp_gain: float32 [768], replicated
- grad_mlp_shift: float32 [768], replicated
- grad_proj_up: float32 [768, 3072], P(None, 'mp')
- grad_bias_up: float32 [3072], P('mp')
- grad_proj_down: float32 [3072, 768], P('mp')
- grad_bias_down: float32 [768], replicated
Inputs may be any that keep to these rules, and one draw needn't show every extreme that they name: Row g gives the lengths of the documents packed in order into group g's 2048 tokens: either one document of 2048 tokens and 0, or two of half of 2048 each; exactly half of the rows hold two documents.
All inputs are finite; a program needn't handle non-finite values.
Results may differ from a plain program's by a relative error of at most 0.024.
Values may be sent and summed in bfloat16 or wider, within the bound.
No kernel may reach another device: no remote copies, remote signals or barrier semaphores. Data moves between devices by JAX's collectives and lax.ppermute only.
A program may use at most 256 MiB of HBM per device.

v0:
```python
from functools import partial
import math
import jax
import jax.numpy as jnp
from jax import lax
from jax.sharding import PartitionSpec as P


def layer_norm(values, scale_vec, shift_vec):
    average = jnp.mean(values, axis=-1, keepdims=True)
    centered = values - average
    variance = jnp.mean(centered * centered, axis=-1, keepdims=True)
    return centered * lax.rsqrt(variance + 1e-05) * scale_vec + shift_vec


def short_mix(first_len, streams, short_taps):
    seq_len = streams.shape[0]
    positions = jnp.arange(seq_len, dtype=jnp.int32)[:, None, None]
    result = short_taps[0] * streams
    for offset in (1, 2):
        shifted = jnp.concatenate(
            [jnp.zeros((offset,) + streams.shape[1:], streams.dtype), streams[:-offset]], axis=0
        )
        valid_mask = (positions >= offset) & (
            (positions < first_len) | (positions - offset >= first_len)
        )
        result = result + valid_mask.astype(streams.dtype) * (short_taps[offset] * shifted)
    return (result[:, 0], result[:, 1] * result[:, 2])


def build_kernel(raw_taps, decay_rates):
    seq_len = raw_taps.shape[0]
    positions = jnp.arange(seq_len).astype(raw_taps.dtype)[:, None]
    decayed = raw_taps * jnp.exp(-decay_rates * positions)
    padded = jnp.pad(decayed, ((1, 1), (0, 0)))
    pooled = (padded[:-2] + padded[1:-1] + padded[2:]) / 3.0
    return jnp.sign(pooled) * jnp.maximum(jnp.abs(pooled) - 0.003, 0.0)


def gate_mix(queries, conv_out, mixed_in, skip_gain):
    return queries * (conv_out + skip_gain * mixed_in)


def gelu_exact(values):
    return jax.nn.gelu(values, approximate=False)


def plain_product(lhs_mat, rhs_mat):
    return jnp.dot(lhs_mat, rhs_mat, preferred_element_type=jnp.float32)


def tall_product(lhs_mat, rhs_mat):
    return lax.dot_general(
        lhs_mat, rhs_mat, (((0,), (0,)), ((), ())), preferred_element_type=jnp.float32
    )


def wide_product(lhs_mat, rhs_mat):
    return lax.dot_general(
        lhs_mat, rhs_mat, (((1,), (1,)), ((), ())), preferred_element_type=jnp.float32
    )


def exact_product(lhs_mat, rhs_mat):
    return jnp.dot(
        lhs_mat, rhs_mat, precision=lax.Precision.HIGHEST, preferred_element_type=jnp.float32
    )


def across(table, values):
    return jnp.einsum(
        "jn,knc->kjc",
        table,
        values,
        precision=lax.Precision.HIGHEST,
        preferred_element_type=jnp.float32,
    )


def dft_pair(out_count, in_count, period):
    outer = lax.iota(jnp.int32, out_count)[:, None]
    inner = lax.iota(jnp.int32, in_count)[None, :]
    angles = (outer * inner % period).astype(jnp.float32) * (2.0 * math.pi / period)
    return (jnp.cos(angles), jnp.sin(angles))


def twiddles(rows_p, cols_q, period):
    outer = lax.iota(jnp.int32, rows_p)[:, None]
    inner = lax.iota(jnp.int32, cols_q)[None, :]
    angles = (outer * inner % period).astype(jnp.float32) * (2.0 * math.pi / period)
    return (jnp.cos(angles)[:, :, None], jnp.sin(angles)[:, :, None])


def split_sizes(seq_len):
    period = 2 * seq_len
    exponent = period.bit_length() - 1
    rows_p = 2 ** ((exponent + 1) // 2)
    return (period, rows_p, period // rows_p)


def spectrum(signal):
    seq_len, columns = signal.shape
    period, rows_p, cols_q = split_sizes(seq_len)
    half = rows_p // 2
    flat = signal.reshape(half, cols_q * columns)
    cos_p, sin_p = dft_pair(rows_p, half, rows_p)
    first_re = exact_product(cos_p, flat).reshape(rows_p, cols_q, columns)
    first_im = -exact_product(sin_p, flat).reshape(rows_p, cols_q, columns)
    turn_cos, turn_sin = twiddles(rows_p, cols_q, period)
    turned_re = first_re * turn_cos + first_im * turn_sin
    turned_im = first_im * turn_cos - first_re * turn_sin
    cos_q, sin_q = dft_pair(cols_q, cols_q, cols_q)
    spec_re = across(cos_q, turned_re) + across(sin_q, turned_im)
    spec_im = across(cos_q, turned_im) - across(sin_q, turned_re)
    return (spec_re, spec_im)


def inverse_real(spec_re, spec_im):
    rows_p, cols_q, columns = spec_re.shape
    period = rows_p * cols_q
    half = rows_p // 2
    cos_q, sin_q = dft_pair(cols_q, cols_q, cols_q)
    back_re = across(cos_q, spec_re) - across(sin_q, spec_im)
    back_im = across(cos_q, spec_im) + across(sin_q, spec_re)
    turn_cos, turn_sin = twiddles(rows_p, cols_q, period)
    turned_re = back_re * turn_cos - back_im * turn_sin
    turned_im = back_im * turn_cos + back_re * turn_sin
    cos_i, sin_i = dft_pair(half, rows_p, rows_p)
    result = exact_product(cos_i, turned_re.reshape(rows_p, cols_q * columns)) - exact_product(
        sin_i, turned_im.reshape(rows_p, cols_q * columns)
    )
    return result.reshape(half * cols_q, columns) / float(period)


def long_conv(mixed_in, kernel, mask_one, mask_two):
    channels = mixed_in.shape[1]
    stacked = jnp.concatenate([mask_one * mixed_in, mask_two * mixed_in, kernel], axis=1)
    spec_re, spec_im = spectrum(stacked)
    sig_re = spec_re[:, :, : 2 * channels]
    sig_im = spec_im[:, :, : 2 * channels]
    ker_re = jnp.tile(spec_re[:, :, 2 * channels :], (1, 1, 2))
    ker_im = jnp.tile(spec_im[:, :, 2 * channels :], (1, 1, 2))
    prod_re = sig_re * ker_re - sig_im * ker_im
    prod_im = sig_re * ker_im + sig_im * ker_re
    totals = inverse_real(prod_re, prod_im)
    return mask_one * totals[:, :channels] + mask_two * totals[:, channels:]


def long_conv_back(grad_conv, mixed_in, kernel, mask_one, mask_two):
    channels = mixed_in.shape[1]
    stacked = jnp.concatenate(
        [
            mask_one * mixed_in,
            mask_two * mixed_in,
            mask_one * grad_conv,
            mask_two * grad_conv,
            kernel,
        ],
        axis=1,
    )
    spec_re, spec_im = spectrum(stacked)
    sig_re = spec_re[:, :, : 2 * channels]
    sig_im = spec_im[:, :, : 2 * channels]
    out_re = spec_re[:, :, 2 * channels : 4 * channels]
    out_im = spec_im[:, :, 2 * channels : 4 * channels]
    ker_re = jnp.tile(spec_re[:, :, 4 * channels :], (1, 1, 2))
    ker_im = jnp.tile(spec_im[:, :, 4 * channels :], (1, 1, 2))
    back_in_re = ker_re * out_re + ker_im * out_im
    back_in_im = ker_re * out_im - ker_im * out_re
    cor_re = sig_re * out_re + sig_im * out_im
    cor_im = sig_re * out_im - sig_im * out_re
    cor_re = cor_re[:, :, :channels] + cor_re[:, :, channels:]
    cor_im = cor_im[:, :, :channels] + cor_im[:, :, channels:]
    totals = inverse_real(
        jnp.concatenate([back_in_re, cor_re], axis=2), jnp.concatenate([back_in_im, cor_im], axis=2)
    )
    grad_mixed = mask_one * totals[:, :channels] + mask_two * totals[:, channels : 2 * channels]
    return (grad_mixed, totals[:, 2 * channels :])


def per_device(
    tokens,
    lengths,
    mix_gain,
    mix_shift,
    proj_in,
    bias_in,
    short_taps,
    long_taps,
    decay_rates,
    skip_gain,
    proj_out,
    bias_out,
    mlp_gain,
    mlp_shift,
    proj_up,
    bias_up,
    proj_down,
    bias_down,
    cotangent,
):
    seq_len, width = tokens.shape
    channels = proj_in.shape[2]
    first_len = lengths[0, 0]
    second_len = lengths[0, 1]
    positions = jnp.arange(seq_len, dtype=jnp.int32)[:, None]
    mask_one = (positions < first_len).astype(jnp.float32)
    mask_two = ((positions >= first_len) & (positions < first_len + second_len)).astype(jnp.float32)
    tokens_f = tokens.astype(jnp.float32)
    normed, norm_pull = jax.vjp(layer_norm, tokens_f, mix_gain, mix_shift)
    normed_low = normed.astype(jnp.bfloat16)
    proj_flat = proj_in.reshape(width, 3 * channels)
    streams = (plain_product(normed_low, proj_flat) + bias_in.reshape(-1)).reshape(
        seq_len, 3, channels
    )
    (queries, mixed_in), short_pull = jax.vjp(partial(short_mix, first_len), streams, short_taps)
    gathered = lax.all_gather(long_taps, "dp", axis=0, tiled=True)
    kernel, kernel_pull = jax.vjp(build_kernel, gathered.astype(jnp.float32), decay_rates)
    conv_out = long_conv(mixed_in, kernel, mask_one, mask_two)
    gated_out, gate_pull = jax.vjp(gate_mix, queries, conv_out, mixed_in, skip_gain)
    gated_low = gated_out.astype(jnp.bfloat16)
    attn_terms = plain_product(gated_low, proj_out)
    attn_out = lax.psum(attn_terms.astype(jnp.bfloat16), "mp").astype(jnp.float32) + bias_out
    hidden_one = tokens_f + attn_out
    normed_two, norm_two_pull = jax.vjp(layer_norm, hidden_one, mlp_gain, mlp_shift)
    normed_two_low = normed_two.astype(jnp.bfloat16)
    pre_act = plain_product(normed_two_low, proj_up) + bias_up
    hidden, gelu_pull = jax.vjp(gelu_exact, pre_act)
    hidden_low = hidden.astype(jnp.bfloat16)
    down_terms = plain_product(hidden_low, proj_down)
    mlp_out = lax.psum(down_terms.astype(jnp.bfloat16), "mp").astype(jnp.float32) + bias_down
    output = (hidden_one + mlp_out).astype(jnp.bfloat16)
    grad_proj_down = tall_product(hidden_low, cotangent)
    grad_bias_down = jnp.sum(cotangent.astype(jnp.float32), axis=0)
    (grad_pre,) = gelu_pull(wide_product(cotangent, proj_down))
    grad_pre_low = grad_pre.astype(jnp.bfloat16)
    grad_proj_up = tall_product(normed_two_low, grad_pre_low)
    grad_bias_up = jnp.sum(grad_pre_low.astype(jnp.float32), axis=0)
    grad_norm_terms = wide_product(grad_pre_low, proj_up)
    cot_f = cotangent.astype(jnp.float32)
    grad_normed_two = lax.psum(grad_norm_terms.astype(jnp.bfloat16), "mp").astype(jnp.float32)
    grad_hidden_part, grad_mlp_gain, grad_mlp_shift = norm_two_pull(grad_normed_two)
    grad_hidden_one = cot_f + grad_hidden_part
    grad_bias_out = jnp.sum(grad_hidden_one, axis=0)
    grad_attn_low = grad_hidden_one.astype(jnp.bfloat16)
    grad_proj_out = tall_product(gated_low, grad_attn_low)
    grad_gated = wide_product(grad_attn_low, proj_out)
    grad_queries, grad_conv, grad_mixed_direct, grad_skip_gain = gate_pull(grad_gated)
    regathered = lax.all_gather(long_taps, "dp", axis=0, tiled=True)
    kernel_back, kernel_pull_back = jax.vjp(
        build_kernel, regathered.astype(jnp.float32), decay_rates
    )
    grad_mixed_conv, grad_kernel = long_conv_back(
        grad_conv, mixed_in, kernel_back, mask_one, mask_two
    )
    grad_taps_full, grad_decay_rates = kernel_pull_back(grad_kernel)
    grad_streams, grad_short_taps = short_pull((grad_queries, grad_mixed_direct + grad_mixed_conv))
    grad_streams_low = grad_streams.reshape(seq_len, 3 * channels).astype(jnp.bfloat16)
    grad_proj_in = tall_product(normed_low, grad_streams_low).reshape(width, 3, channels)
    grad_bias_in = jnp.sum(grad_streams_low.astype(jnp.float32), axis=0).reshape(3, channels)
    grad_normed = lax.psum(
        wide_product(grad_streams_low, proj_flat).astype(jnp.bfloat16), "mp"
    ).astype(jnp.float32)
    grad_tokens_part, grad_mix_gain, grad_mix_shift = norm_pull(grad_normed)
    input_grad = grad_hidden_one + grad_tokens_part
    grad_long_taps = lax.psum_scatter(
        grad_taps_full.astype(jnp.bfloat16), "dp", scatter_dimension=0, tiled=True
    ).astype(jnp.float32)
    (
        grad_mix_gain,
        grad_mix_shift,
        grad_proj_in,
        grad_bias_in,
        grad_short_taps,
        grad_decay_rates,
        grad_skip_gain,
        grad_proj_out,
        grad_bias_out,
        grad_mlp_gain,
        grad_mlp_shift,
        grad_proj_up,
        grad_bias_up,
        grad_proj_down,
        grad_bias_down,
    ) = (
        lax.psum(grad_mix_gain.astype(jnp.bfloat16), "dp").astype(jnp.float32),
        lax.psum(grad_mix_shift.astype(jnp.bfloat16), "dp").astype(jnp.float32),
        lax.psum(grad_proj_in.astype(jnp.bfloat16), "dp").astype(jnp.float32),
        lax.psum(grad_bias_in.astype(jnp.bfloat16), "dp").astype(jnp.float32),
        lax.psum(grad_short_taps.astype(jnp.bfloat16), "dp").astype(jnp.float32),
        lax.psum(grad_decay_rates.astype(jnp.bfloat16), "dp").astype(jnp.float32),
        lax.psum(grad_skip_gain.astype(jnp.bfloat16), "dp").astype(jnp.float32),
        lax.psum(grad_proj_out.astype(jnp.bfloat16), "dp").astype(jnp.float32),
        lax.psum(grad_bias_out.astype(jnp.bfloat16), "dp").astype(jnp.float32),
        lax.psum(grad_mlp_gain.astype(jnp.bfloat16), "dp").astype(jnp.float32),
        lax.psum(grad_mlp_shift.astype(jnp.bfloat16), "dp").astype(jnp.float32),
        lax.psum(grad_proj_up.astype(jnp.bfloat16), "dp").astype(jnp.float32),
        lax.psum(grad_bias_up.astype(jnp.bfloat16), "dp").astype(jnp.float32),
        lax.psum(grad_proj_down.astype(jnp.bfloat16), "dp").astype(jnp.float32),
        lax.psum(grad_bias_down.astype(jnp.bfloat16), "dp").astype(jnp.float32),
    )
    return (
        output,
        input_grad,
        grad_mix_gain,
        grad_mix_shift,
        grad_proj_in,
        grad_bias_in,
        grad_short_taps,
        grad_long_taps,
        grad_decay_rates,
        grad_skip_gain,
        grad_proj_out,
        grad_bias_out,
        grad_mlp_gain,
        grad_mlp_shift,
        grad_proj_up,
        grad_bias_up,
        grad_proj_down,
        grad_bias_down,
    )


def solution(mesh):
    in_specs = (
        P("dp", None),
        P("dp", None),
        P(),
        P(),
        P(None, None, "mp"),
        P(None, "mp"),
        P(None, None, "mp"),
        P("dp", "mp"),
        P("mp"),
        P("mp"),
        P("mp", None),
        P(),
        P(),
        P(),
        P(None, "mp"),
        P("mp"),
        P("mp", None),
        P(),
        P("dp", None),
    )
    out_specs = (
        P("dp", None),
        P("dp", None),
        P(),
        P(),
        P(None, None, "mp"),
        P(None, "mp"),
        P(None, None, "mp"),
        P("dp", "mp"),
        P("mp"),
        P("mp"),
        P("mp", None),
        P(),
        P(),
        P(),
        P(None, "mp"),
        P("mp"),
        P("mp", None),
        P(),
    )
    return jax.shard_map(
        per_device, mesh=mesh, in_specs=in_specs, out_specs=out_specs, check_vma=False
    )
```

profile of v0, /device:TPU:0, one launch (start us, length us, event | category | flops | bytes accessed | tf_op | source)
XLA Modules:
  0.0 1298.6 jit_solution(12647565833582045572)
XLA Ops:
  19.3 33.9 %all_gather.4 = bf16[2048,192]{0,1:T(8,128)(2,1)S(1)} all-gather(bf16[256,192]{0,1:T(8,128)(2,1)S(1)} %copy-done.53), channel_id=1, replica_groups=mesh['dp'=8,'mp'=4] {'dp'}, dimensions={0}, use_global_device_ids=true | all-gather | bytes 884736 | tf_op jit(solution)/shard_map/all_gather | solution.py:217
  69.1 5.8 copy.51
  74.9 6.4 reshape.291
  81.2 6.4 dot_general.122
  87.6 16.4 %fusion.51 = f32[64,64,576]{2,0,1:T(8,128)} fusion(f32[64,576,32]{1,0,2:T(8,128)} %dot_general.122), kind=kOutput, calls=%fused_computation.95 | convolution fusion | flops 905998336 | bytes 14155776 | tf_op jit(solution)/shard_map/dot_general | solution.py:65
  104.1 20.2 %multiply_add_fusion.1 = (f32[64,64,576]{2,0,1:T(8,128)}, f32[64,64,576]{2,0,1:T(8,128)S(1)}) fusion(f32[64,64,576]{2,0,1:T(8,128)} %fusion.51, f32[64,64]{0,1:T(8,128)S(1)} %copy.55, f32[64,64]{0,1:T(8,128)S(1)} %copy.53, f32[64,576,32]{1,0,2:T(8,128)} %dot_general.122), kind=kOutput, calls=%fused_computation.23 | convolution fusion | flops 922513408 | bytes 33062912 | tf_op jit(solution)/shard_map/dot_general | solution.py:65
  124.3 21.2 %fusion.10 = f32[64,576,64]{1,2,0:T(8,128)} fusion(f32[64,64,576]{2,0,1:T(8,128)S(1)} %get-tuple-element.76), kind=kOutput, calls=%fused_computation.24 | convolution fusion | flops 1811996672 | bytes 18874368 | tf_op jit(solution)/shard_map/jn,knc->kjc/dot_general | solution.py:71
  145.5 21.2 %fusion.12 = f32[64,576,64]{1,2,0:T(8,128)} fusion(f32[64,64,576]{2,0,1:T(8,128)S(1)} %get-tuple-element.76), kind=kOutput, calls=%fused_computation.26 | convolution fusion | flops 1811996672 | bytes 18874368 | tf_op jit(solution)/shard_map/jn,knc->kjc/dot_general | solution.py:71
  166.7 23.6 %subtract_bitcast_fusion.2 = f32[64,64,576]{2,1,0:T(8,128)} fusion(f32[64,576,64]{1,2,0:T(8,128)} %fusion.10, f32[64,64,576]{2,0,1:T(8,128)} %get-tuple-element.75), kind=kOutput, calls=%fused_computation.20 | convolution fusion | flops 1814355968 | bytes 28311552 | tf_op jit(solution)/shard_map/jn,knc->kjc/dot_general | solution.py:71
  190.3 22.4 %add_bitcast_fusion.2 = f32[64,64,576]{2,1,0:T(8,128)S(1)} fusion(f32[64,576,64]{1,2,0:T(8,128)} %fusion.12, f32[64,64,576]{2,0,1:T(8,128)} %get-tuple-element.75), kind=kOutput, calls=%fused_computation.21 | convolution fusion | flops 1814355968 | bytes 28311552 | tf_op jit(solution)/shard_map/jn,knc->kjc/dot_general | solution.py:71
  217.0 4.5 tile.16
  221.5 10.7 tile.17
  234.4 4.4 tile.18
  238.8 11.1 tile.19
  249.9 9.6 multiply_subtract_fusion.5
  259.6 7.9 fusion.93
  267.4 7.8 fusion.105
  275.2 7.9 fusion.95
  283.1 14.9 %multiply_add_fusion.4 = (f32[64,384,64]{1,2,0:T(8,128)}, f32[64,384,64]{1,2,0:T(8,128)}) fusion(f32[64,64]{1,0:T(8,128)S(1)} %get-tuple-element.98, f32[64,64]{1,0:T(8,128)S(1)} %get-tuple-element.99, f32[64,384,64]{1,2,0:T(8,128)} %fusion.93, f32[64,384,64]{1,2,0:T(8,128)} %fusion.105, f32[64,384,64]{1,2,0:T(8,128)} %fusion.95, ...), kind=kOutput, calls=%fused_computation.90 | convolution fusion | flops 1220599808 | bytes 37781504 | tf_op jit(solution)/shard_map/jn,knc->kjc/dot_general | solution.py:71
  298.0 6.5 copy.80
  311.7 5.5 fusion.1
  320.4 4.9 fusion.291
  338.8 69.5 %all-reduce.22.cloned.1.call-done = bf16[2048,768]{1,0:T(8,128)(2,1)} async-done(((bf16[2048,768]{1,0:T(8,128)(2,1)}), bf16[2048,768]{1,0:T(8,128)(2,1)}) %all-reduce.22.cloned.1.call-update) | async-done | bytes 3145744 | tf_op jit(solution)/shard_map/psum | solution.py:223
  419.0 19.1 %fusion.283 = (bf16[768]{0:T(1024)(128)(2,1)}, bf16[2048,768]{1,0:T(8,128)(2,1)S(1)}, f32[2048,768]{1,0:T(8,128)}) fusion(f32[2048,768]{1,0:T(8,128)S(1)} %fusion.278, f32[768]{0:T(1024)S(1)} %copy-done.82, bf16[2048,768]{1,0:T(8,128)(2,1)S(1)} %copy-done.24, bf16[768,768]{1,0:T(8,128)(2,1)S(1)} %copy-done), kind=kOutput, calls=%fused_computation.369 | convolution fusion | flops 2532310272 | bytes 20058624 | tf_op jit(solution)/shard_map/dot_general | solution.py:59
  443.8 5.5 multiply_convert_fusion
  455.4 57.0 %all-reduce.24.cloned.1.call-done = bf16[2048,768]{1,0:T(8,128)(2,1)} async-done(((bf16[2048,768]{1,0:T(8,128)(2,1)}), bf16[2048,768]{1,0:T(8,128)(2,1)}) %all-reduce.24.cloned.1.call-update) | async-done | bytes 3145744 | tf_op jit(solution)/shard_map/psum | solution.py:241
  512.4 5.6 fusion.40
  518.9 5.2 fusion.41
  528.5 5.6 multiply_reduce_fusion.4
  538.9 9.2 copy.62
  548.1 9.1 reshape.294
  557.1 8.9 dot_general.142
  566.0 25.4 %fusion.30 = f32[64,64,960]{2,0,1:T(8,128)} fusion(f32[64,960,32]{1,0,2:T(8,128)} %dot_general.142), kind=kOutput, calls=%fused_computation.46 | convolution fusion | flops 1509978112 | bytes 23592960 | tf_op jit(solution)/shard_map/dot_general | solution.py:65
  591.4 26.6 %multiply_add_fusion = (f32[64,64,960]{2,0,1:T(8,128)}, f32[64,64,960]{2,0,1:T(8,128)}) fusion(f32[64,64,960]{2,0,1:T(8,128)} %fusion.30, f32[64,64]{0,1:T(8,128)S(1)} %copy-done.40, f32[64,64]{0,1:T(8,128)S(1)} %copy-done.42, f32[64,960,32]{1,0,2:T(8,128)S(1)} %copy-done.10), kind=kOutput, calls=%fused_computation.7 | convolution fusion | flops 1537503232 | bytes 55083008 | tf_op jit(solution)/shard_map/dot_general | solution.py:65
  618.0 36.1 %fusion.2 = f32[64,960,64]{1,2,0:T(8,128)} fusion(f32[64,64,960]{2,0,1:T(8,128)} %get-tuple-element.68), kind=kOutput, calls=%fused_computation.8 | convolution fusion | flops 3019956224 | bytes 31457280 | tf_op jit(solution)/shard_map/jn,knc->kjc/dot_general | solution.py:71
  654.1 36.5 %fusion.4 = f32[64,960,64]{1,2,0:T(8,128)} fusion(f32[64,64,960]{2,0,1:T(8,128)} %get-tuple-element.68), kind=kOutput, calls=%fused_computation.10 | convolution fusion | flops 3019956224 | bytes 31457280 | tf_op jit(solution)/shard_map/jn,knc->kjc/dot_general | solution.py:71
  690.6 32.7 %subtract_bitcast_fusion = f32[64,64,960]{2,1,0:T(8,128)} fusion(f32[64,960,64]{1,2,0:T(8,128)} %fusion.2, f32[64,64,960]{2,0,1:T(8,128)} %get-tuple-element.67), kind=kOutput, calls=%fused_computation.4 | convolution fusion | flops 3023888384 | bytes 47185920 | tf_op jit(solution)/shard_map/jn,knc->kjc/dot_general | solution.py:71
  723.3 32.6 %add_bitcast_fusion = f32[64,64,960]{2,1,0:T(8,128)} fusion(f32[64,960,64]{1,2,0:T(8,128)} %fusion.4, f32[64,64,960]{2,0,1:T(8,128)} %get-tuple-element.67), kind=kOutput, calls=%fused_computation.5 | convolution fusion | flops 3023888384 | bytes 47185920 | tf_op jit(solution)/shard_map/jn,knc->kjc/dot_general | solution.py:71
  758.1 4.5 tile.40
  762.6 10.7 tile.41
  775.5 4.4 tile.42
  780.0 10.7 tile.43
  790.7 23.6 %multiply_add_fusion.3 = (f32[64,64,384]{2,1,0:T(8,128)}, f32[64,64,384]{2,1,0:T(8,128)}, f32[64,64,384]{2,1,0:T(8,128)}, f32[64,64,384]{2,1,0:T(8,128)}) fusion(f32[64,64,384]{2,1,0:T(8,128)} %tile.43, f32[64,64,384]{2,1,0:T(8,128)} %tile.41, f32[64,64,960]{2,1,0:T(8,128)} %subtract_bitcast_fusion, f32[64,64,960]{2,1,0:T(8,128)} %add_bitcast_fusion), kind=kLoop, calls=%fused_computation.71 | loop fusion | flops 18874368 | bytes 62914560 | tf_op jit(solution)/shard_map/add | solution.py:168
  814.3 4.7 slice_add_fusion
  819.5 12.4 fusion.26
  831.9 12.7 fusion.27
  844.6 4.6 slice_add_fusion.1
  851.2 12.4 fusion.28
  863.6 28.0 %add_bitcast_fusion.1 = (f32[64,64,576]{2,1,0:T(8,128)}, f32[64,64,576]{2,1,0:T(8,128)}) fusion(f32[64,64]{1,0:T(8,128)S(1)} %copy-done.36, f32[64,64]{1,0:T(8,128)S(1)} %copy-done.38, f32[64,576,64]{1,2,0:T(8,128)} %fusion.26, f32[64,576,64]{1,2,0:T(8,128)} %fusion.28, f32[64,576,64]{1,2,0:T(8,128)} %fusion.27, f32[64,64,192]{2,1,0:T(8,128)} %copy-done.16, ...), kind=kOutput, calls=%fused_computation.18 | convolution fusion | flops 1833230336 | bytes 56655872 | tf_op jit(solution)/shard_map/jn,knc->kjc/dot_general | solution.py:71
  891.6 11.9 reshape.296
  903.5 11.9 reshape.295
  915.5 7.7 fusion.160
  923.1 6.8 fusion
  929.9 6.6 div.72
  936.5 6.6 fusion.290
  961.0 5.3 multiply_reduce_fusion.3
  975.0 6.7 convolution_convert_fusion.3
  981.8 7.5 convolution_convert_fusion.4
  999.6 14.3 %reduce-scatter.2.cloned.1.call-done = bf16[256,192]{0,1:T(8,128)(2,1)} async-done(((bf16[2048,192]{0,1:T(8,128)(2,1)}), bf16[256,192]{0,1:T(8,128)(2,1)}) %reduce-scatter.2.cloned.1.call-update) | async-done | bytes 98320 | tf_op jit(solution)/shard_map/reduce_scatter | solution.py:266
  1015.5 120.2 %all-reduce.28.cloned.1.call-done = (bf16[2048,768]{1,0:T(8,128)(2,1)}, bf16[2048,768]{1,0:T(8,128)(2,1)}) async-done(((bf16[2048,768]{1,0:T(8,128)(2,1)}, bf16[2048,768]{1,0:T(8,128)(2,1)}), (bf16[2048,768]{1,0:T(8,128)(2,1)}, bf16[2048,768]{1,0:T(8,128)(2,1)})) %all-reduce.28.cloned.1.call-update) | async-done | bytes 6291472 | tf_op jit(solution)/shard_map/psum | solution.py:231
  1142.3 5.1 fusion.42
  1147.4 39.5 %all-reduce.14 = (bf16[768]{0:T(1024)(128)(2,1)S(1)}, bf16[768]{0:T(1024)(128)(2,1)S(1)}, bf16[3,192]{1,0:T(4,128)(2,1)S(1)}, bf16[3,3,192]{2,1,0:T(4,128)(2,1)S...) all-reduce(bf16[768]{0:T(1024)(128)(2,1)S(1)} %get-tuple-element.20, ...), channel_id=1, replica_groups=mesh['dp'=8,'mp'=4] {'dp'}, use_global_device_ids=true, to_apply=%region_13.14 | all-reduce | flops 8064 | bytes 32256 | tf_op jit(solution)/shard_map/psum | solution.py:286
  1193.4 12.7 add_add_fusion.2
  1206.1 76.8 %all-reduce.26.cloned.1.call-done = (bf16[768,3,192]{0,2,1:T(8,128)(2,1)}, bf16[192,768]{1,0:T(8,128)(2,1)}, bf16[768,768]{1,0:T(8,128)(2,1)}, bf16[768,768]{1,0:T(8,128)(2,1)}) async-done(((bf16[768,3,192]{0,2,1:T(8,128)(2,1)}, bf16[192,768]{1,0:T(8,128)(2,1)}, bf16[768,768]{1,0:T(8,128)(2,1)}, bf16[768,768]{1,0:T(8,128)(2,1)}), (bf16[768,3,192]{0,2,1:T(8,128)(2,1)}, bf16[192,768]{1,0:T(8,128)(2,1)}, ...) | async-done | bytes 3538960 | tf_op jit(solution)/shard_map/psum | solution.py:288
  (305 shorter events, 155.9 us)
Async XLA Ops:
  7.2 411.7 %copy-start = (bf16[768,768]{1,0:T(8,128)(2,1)S(1)}, bf16[768,768]{1,0:T(8,128)(2,1)}, u32[]{:S(2)}) copy-start(bf16[768,768]{1,0:T(8,128)(2,1)} %param.35) | copy-start | bytes 3538948
  7.2 11.9 copy-start.77
  7.2 12.1 copy-start.53
  7.2 401.1 %all-reduce.22.cloned.1.call-start = ((), (), s32[]{:S(2)}) async-start(), calls=%async_computation.1 | async-start | bytes 6291456 | tf_op jit(solution)/shard_map/psum | solution.py:223
  7.3 49.2 %copy-start.57 = (f32[2048]{0:T(1024)}, f32[2048]{0:T(1024)S(1)}, u32[]{:S(2)}) copy-start(f32[2048]{0:T(1024)S(1)} %iota_convert_fusion) | copy-start | bytes 24580
  9.3 49.7 %copy-start.63 = (f32[2048]{0:T(1024)}, f32[2048]{0:T(1024)S(1)}, u32[]{:S(2)}) copy-start(f32[2048]{0:T(1024)S(1)} %fusion.172) | copy-start | bytes 24580
  10.0 49.0 %copy-start.65 = (f32[2048]{0:T(1024)}, f32[2048]{0:T(1024)S(1)}, u32[]{:S(2)}) copy-start(f32[2048]{0:T(1024)S(1)} %get-tuple-element.97) | copy-start | bytes 24580
  10.0 524.2 %copy-start.45 = (f32[2048]{0:T(1024)}, f32[2048]{0:T(1024)S(1)}, u32[]{:S(2)}) copy-start(f32[2048]{0:T(1024)S(1)} %get-tuple-element.96) | copy-start | bytes 24580
  10.1 273.0 %copy-start.35 = (f32[64,64]{1,0:T(8,128)}, f32[64,64]{1,0:T(8,128)S(1)}, u32[]{:S(2)}) copy-start(f32[64,64]{1,0:T(8,128)S(1)} %get-tuple-element.98) | copy-start | bytes 49156
  10.1 273.0 %copy-start.37 = (f32[64,64]{1,0:T(8,128)}, f32[64,64]{1,0:T(8,128)S(1)}, u32[]{:S(2)}) copy-start(f32[64,64]{1,0:T(8,128)S(1)} %get-tuple-element.99) | copy-start | bytes 49156
  10.9 45.6 %copy-start.78 = (f32[192]{0:T(256)}, f32[192]{0:T(256)S(1)}, u32[]{:S(2)}) copy-start(f32[192]{0:T(256)S(1)} %neg.29) | copy-start | bytes 2308
  13.6 521.9 %copy-start.47 = (f32[2048]{0:T(1024)}, f32[2048]{0:T(1024)S(1)}, u32[]{:S(2)}) copy-start(f32[2048]{0:T(1024)S(1)} %fusion.174) | copy-start | bytes 24580
  16.0 40.5 %copy-start.69 = (f32[768]{0:T(1024)S(1)}, f32[768]{0:T(1024)}, u32[]{:S(2)}) copy-start(f32[768]{0:T(1024)} %param.21) | copy-start | bytes 9220
  16.0 40.5 %copy-start.89 = (bf16[768,3,192]{0,2,1:T(8,128)(2,1)S(1)}, bf16[768,3,192]{0,2,1:T(8,128)(2,1)}, u32[]{:S(2)}) copy-start(bf16[768,3,192]{0,2,1:T(8,128)(2,1)} %param.23) | copy-start | bytes 2654212
  16.0 40.5 %copy-start.93 = (f32[768]{0:T(1024)S(1)}, f32[768]{0:T(1024)}, u32[]{:S(2)}) copy-start(f32[768]{0:T(1024)} %param.22) | copy-start | bytes 9220
  16.0 42.9 %copy-start.43 = (f32[2048]{0:T(1024)}, f32[2048]{0:T(1024)S(1)}, u32[]{:S(2)}) copy-start(f32[2048]{0:T(1024)S(1)} %broadcast_multiply_fusion.5) | copy-start | bytes 24580
  19.0 39.9 %copy-start.61 = (f32[2048]{0:T(1024)}, f32[2048]{0:T(1024)S(1)}, u32[]{:S(2)}) copy-start(f32[2048]{0:T(1024)S(1)} %fusion.43) | copy-start | bytes 24580
  19.1 39.8 %copy-start.54 = (f32[2048]{0:T(1024)}, f32[2048]{0:T(1024)S(1)}, u32[]{:S(2)}) copy-start(f32[2048]{0:T(1024)S(1)} %fusion.175) | copy-start | bytes 24580
  19.1 39.9 %copy-start.71 = (f32[3,192]{1,0:T(4,128)}, f32[3,192]{1,0:T(4,128)S(1)}, u32[]{:S(2)}) copy-start(f32[3,192]{1,0:T(4,128)S(1)} %get-tuple-element.91) | copy-start | bytes 6916
  19.1 39.9 %copy-start.73 = (f32[3,192]{1,0:T(4,128)}, f32[3,192]{1,0:T(4,128)S(1)}, u32[]{:S(2)}) copy-start(f32[3,192]{1,0:T(4,128)S(1)} %get-tuple-element.93) | copy-start | bytes 6916
  19.1 39.9 %copy-start.75 = (f32[3,192]{1,0:T(4,128)}, f32[3,192]{1,0:T(4,128)S(1)}, u32[]{:S(2)}) copy-start(f32[3,192]{1,0:T(4,128)S(1)} %get-tuple-element.92) | copy-start | bytes 6916
  19.2 84.9 %copy-start.39 = (f32[64,64]{0,1:T(8,128)}, f32[64,64]{0,1:T(8,128)S(1)}, u32[]{:S(2)}) copy-start(f32[64,64]{0,1:T(8,128)S(1)} %copy.55) | copy-start | bytes 49156
  19.3 84.8 %copy-start.41 = (f32[64,64]{0,1:T(8,128)}, f32[64,64]{0,1:T(8,128)S(1)}, u32[]{:S(2)}) copy-start(f32[64,64]{0,1:T(8,128)S(1)} %copy.53) | copy-start | bytes 49156
  19.3 37.2 %copy-start.2 = (bf16[2048,768]{1,0:T(8,128)(2,1)S(1)}, bf16[2048,768]{1,0:T(8,128)(2,1)}, u32[]{:S(2)}) copy-start(bf16[2048,768]{1,0:T(8,128)(2,1)} %param.19) | copy-start | bytes 9437188
  320.4 10.4 copy-start.84
  328.1 7.9 copy-start.34
  335.1 73.2 %copy-start.51 = (f32[768]{0:T(1024)S(1)}, f32[768]{0:T(1024)}, u32[]{:S(2)}) copy-start(f32[768]{0:T(1024)} %param.30) | copy-start | bytes 9220
  338.7 76.3 %copy-start.67 = (f32[768]{0:T(1024)S(1)}, f32[768]{0:T(1024)}, u32[]{:S(2)}) copy-start(f32[768]{0:T(1024)} %param.31) | copy-start | bytes 9220
  338.7 76.3 %copy-start.91 = (f32[768]{0:T(1024)S(1)}, f32[768]{0:T(1024)}, u32[]{:S(2)}) copy-start(f32[768]{0:T(1024)} %param.32) | copy-start | bytes 9220
  338.7 173.7 %all-reduce.24.cloned.1.call-start = ((), (), s32[]{:S(2)}) async-start(), calls=%async_computation.2 | async-start | bytes 6291456 | tf_op jit(solution)/shard_map/psum | solution.py:241
  413.0 111.2 %copy-start.49 = (f32[2048]{0:T(1024)}, f32[2048]{0:T(1024)S(1)}, u32[]{:S(2)}) copy-start(f32[2048]{0:T(1024)S(1)} %broadcast_multiply_fusion.4) | copy-start | bytes 24580
  415.0 109.1 %copy-start.59 = (f32[2048]{0:T(1024)}, f32[2048]{0:T(1024)S(1)}, u32[]{:S(2)}) copy-start(f32[2048]{0:T(1024)S(1)} %fusion.176) | copy-start | bytes 24580
  419.0 19.1 %copy-start.30 = (f32[2048,768]{1,0:T(8,128)}, f32[2048,768]{1,0:T(8,128)S(1)}, u32[]{:S(2)}) copy-start(f32[2048,768]{1,0:T(8,128)S(1)} %fusion.278) | copy-start | bytes 18874372
  443.7 570.2 %reduce-scatter.2.cloned.1.call-start = ((), (), s32[]{:S(2)}) async-start(), calls=%async_computation.3 | async-start | bytes 884736 | tf_op jit(solution)/shard_map/reduce_scatter | solution.py:266
  566.0 25.4 %copy-start.10 = (f32[64,960,32]{1,0,2:T(8,128)S(1)}, f32[64,960,32]{1,0,2:T(8,128)}, u32[]{:S(2)}) copy-start(f32[64,960,32]{1,0,2:T(8,128)} %dot_general.142) | copy-start | bytes 23592964
  566.0 25.4 %copy-start.40 = (f32[64,64]{0,1:T(8,128)S(1)}, f32[64,64]{0,1:T(8,128)}, u32[]{:S(2)}) copy-start(f32[64,64]{0,1:T(8,128)} %copy-done.39) | copy-start | bytes 49156
  566.0 25.4 %copy-start.42 = (f32[64,64]{0,1:T(8,128)S(1)}, f32[64,64]{0,1:T(8,128)}, u32[]{:S(2)}) copy-start(f32[64,64]{0,1:T(8,128)} %copy-done.41) | copy-start | bytes 49156
  819.5 31.6 %slice-start.6 = ((s8[6291456]{0:T(1024)(128)(4,1)}), s8[4194304]{0:T(1024)(128)(4,1)S(1)}, s32[]{:S(2)}) async-start(s8[6291456]{0:T(1024)(128)(4,1)} %bitcast.171), calls=%async_computation.12 | async-start | bytes 8388608
  831.9 19.2 %slice-start.7 = ((s8[6291456]{0:T(1024)(128)(4,1)}), s8[2097152]{0:T(1024)(128)(4,1)S(1)}, s32[]{:S(2)}) async-start(s8[6291456]{0:T(1024)(128)(4,1)} %bitcast.171), calls=%async_computation.13 | async-start | bytes 4194304
  851.1 12.5 copy-start.36
  851.2 12.5 copy-start.38
  915.5 7.7 copy-start.17
  936.5 9.5 copy-start.22
  948.5 7.6 copy-start.20
  948.5 7.6 copy-start.46
  948.5 7.6 copy-start.48
  948.5 7.6 copy-start.85
  950.4 185.2 %all-reduce.28.cloned.1.call-start = ((), (), s32[]{:S(2)}) async-start(), calls=%async_computation.5 | async-start | bytes 12582912 | tf_op jit(solution)/shard_map/psum | solution.py:231
  953.3 7.7 slice-start
  974.7 7.0 copy-start.68
  974.7 7.0 copy-start.92
  974.8 308.2 %all-reduce.26.cloned.1.call-start = ((), (), s32[]{:S(2)}) async-start(), calls=%async_computation.4 | async-start | bytes 7077888 | tf_op jit(solution)/shard_map/psum | solution.py:288
  975.0 14.3 %slice-start.2 = ((s8[6291456]{0:T(1024)(128)(4,1)}), s8[4194304]{0:T(1024)(128)(4,1)S(1)}, s32[]{:S(2)}) async-start(s8[6291456]{0:T(1024)(128)(4,1)} %bitcast.169), calls=%async_computation.8 | async-start | bytes 8388608
  981.8 7.6 slice-start.3
  981.8 7.6 copy-start.27
  997.2 145.1 %copy-start.62 = (f32[2048]{0:T(1024)S(1)}, f32[2048]{0:T(1024)}, u32[]{:S(2)}) copy-start(f32[2048]{0:T(1024)} %copy-done.61) | copy-start | bytes 24580
  1138.1 9.3 copy-start.80
  1138.1 9.3 copy-start.81
  1138.1 9.3 copy-start.86
  1138.1 9.3 copy-start.87
  1138.1 55.3 %copy-start.56 = (f32[2048]{0:T(1024)S(1)}, f32[2048]{0:T(1024)}, u32[]{:S(2)}) copy-start(f32[2048]{0:T(1024)} %copy-done.54) | copy-start | bytes 24580
  1138.1 55.3 %copy-start.83 = (f32[768]{0:T(1024)S(1)}, f32[768]{0:T(1024)}, u32[]{:S(2)}) copy-start(f32[768]{0:T(1024)} %param.36) | copy-start | bytes 9220
  1193.4 98.4 %copy-start.1 = (bf16[768,768]{1,0:T(8,128)(2,1)S(1)}, bf16[768,768]{1,0:T(8,128)(2,1)}, u32[]{:S(2)}) copy-start(bf16[768,768]{1,0:T(8,128)(2,1)} %param.35) | copy-start | bytes 3538948
  1282.9 7.3 copy-start.33
  (47 other events, 186.1 us)
Sparse Core Ops, SparseCore 0:
  338.8 69.4 all-reduce.21
  443.8 68.5 all-reduce.23
  950.6 63.2 reduce-scatter.1
  1016.8 118.7 all-reduce.27
  1141.7 141.1 all-reduce.25
where the time goes:
time: 1310 us; the launch traced here: 1300 us
  matrix products  508 us (39%)
  waiting for transfers between devices  338 us (26%)
  local copies, waits for them, and re-layouts  199 us (15%)
  other arithmetic  163 us (12%)
  blocking collectives  73.4 us (6%)
  between operations  16.7 us (1%)
    dot_general x16, matrix products, across(): jnp.einsum('jn,knc->kjc', table, values, precision=lax.Precision.HIGHEST,...  330 us
    psum x1, waiting for transfers between devices, per_device(): lax.psum(down_terms.astype(jnp.bfloat16), 'mp').astype(jnp.float32)  120 us
    dot_general x8, matrix products, exact_product(): jnp.dot(lhs_mat, rhs_mat, precision=lax.Precision.HIGHEST, preferred_elem...  112 us
    psum x1, waiting for transfers between devices, per_device(): lax.psum(grad_proj_in.astype(jnp.bfloat16), 'dp').astype(jnp.float32)  76.8 us
    psum x1, waiting for transfers between devices, per_device(): lax.psum(attn_terms.astype(jnp.bfloat16), 'mp').astype(jnp.float32)  69.5 us
    psum x1, waiting for transfers between devices, per_device(): lax.psum(grad_norm_terms.astype(jnp.bfloat16), 'mp').astype(jnp.float32)  57 us
    psum x1, blocking collectives, per_device(): lax.psum(grad_mix_gain.astype(jnp.bfloat16), 'dp').astype(jnp.float32)  39.5 us
    unnamed x213, local copies, waits for them, and re-layouts  38.2 us
  transfers between devices with their start and end apart: 5, of which 5 were waited for; matrix products, arithmetic and copies ran while one was open for 7% of the time, Pallas kernels for 0%

commit v1 on v0

--- a/solution.py
+++ b/solution.py
@@ -214,7 +214,12 @@
         seq_len, 3, channels
     )
     (queries, mixed_in), short_pull = jax.vjp(partial(short_mix, first_len), streams, short_taps)
-    gathered = lax.all_gather(long_taps, "dp", axis=0, tiled=True)
+    ring = [long_taps]
+    for hop in range(7):
+        ring.append(lax.ppermute(ring[-1], "dp", [(dev, (dev + 1) % 8) for dev in range(8)]))
+    gathered = jnp.roll(
+        jnp.concatenate(ring[::-1], axis=0), (lax.axis_index("dp") + 1) * ring[0].shape[0], axis=0
+    )
     kernel, kernel_pull = jax.vjp(build_kernel, gathered.astype(jnp.float32), decay_rates)
     conv_out = long_conv(mixed_in, kernel, mask_one, mask_two)
     gated_out, gate_pull = jax.vjp(gate_mix, queries, conv_out, mixed_in, skip_gain)

time: 1310 us -> 1350 us (1.031)
  waiting for transfers between devices: 338 us -> 357 us
  local copies, waits for them, and re-layouts: 199 us -> 214 us
    ppermute x0 -> x7, waiting for transfers between devices: none -> 23.3 us  [per_device(): lax.ppermute(ring[-1], 'dp', [(dev, (dev + 1) % 8) for dev in range(8)])]
    unnamed x213 -> x234, local copies, waits for them, and re-layouts: 38.2 us -> 49.6 us
  transfers between devices with their start and end apart: 5 -> 12, of which waited for: 5 -> 10; matrix products, arithmetic and copies ran while one was open for 7% -> 9% of each run, Pallas kernels for 0% -> 0%
where the time goes in v1:
time: 1350 us; the launch traced here: 1340 us
  matrix products  507 us (38%)
  waiting for transfers between devices  357 us (26%)
  local copies, waits for them, and re-layouts  214 us (16%)
  other arithmetic  167 us (12%)
  blocking collectives  72.6 us (5%)
  between operations  16.7 us (1%)
    dot_general x16, matrix products, across(): jnp.einsum('jn,knc->kjc', table, values, precision=lax.Precision.HIGHEST,...  330 us
    psum x1, waiting for transfers between devices, per_device(): lax.psum(down_terms.astype(jnp.bfloat16), 'mp').astype(jnp.float32)  120 us
    dot_general x8, matrix products, exact_product(): jnp.dot(lhs_mat, rhs_mat, precision=lax.Precision.HIGHEST, preferred_elem...  112 us
    psum x1, waiting for transfers between devices, per_device(): lax.psum(grad_proj_in.astype(jnp.bfloat16), 'dp').astype(jnp.float32)  76.8 us
    psum x1, waiting for transfers between devices, per_device(): lax.psum(attn_terms.astype(jnp.bfloat16), 'mp').astype(jnp.float32)  65.8 us
    psum x1, waiting for transfers between devices, per_device(): lax.psum(grad_norm_terms.astype(jnp.bfloat16), 'mp').astype(jnp.float32)  57 us
    unnamed x234, local copies, waits for them, and re-layouts  49.6 us
    psum x1, blocking collectives, per_device(): lax.psum(grad_mix_gain.astype(jnp.bfloat16), 'dp').astype(jnp.float32)  39.5 us
  transfers between devices with their start and end apart: 12, of which 10 were waited for; matrix products, arithmetic and copies ran while one was open for 9% of the time, Pallas kernels for 0%

profile of v1, /device:TPU:0, one launch (start us, length us, event | category | flops | bytes accessed | tf_op | source)
XLA Modules:
  0.0 1342.4 jit_solution(11296070064207859223)
XLA Ops:
  33.6 6.6 collective-permute-done.2
  42.2 5.4 collective-permute-done.3
  47.7 33.1 %all_gather.3 = bf16[2048,192]{0,1:T(8,128)(2,1)S(1)} all-gather(bf16[256,192]{0,1:T(8,128)(2,1)} %param.26), channel_id=1, replica_groups=mesh['dp'=8,'mp'=4] {'dp'}, dimensions={0}, use_global_device_ids=true | all-gather | bytes 884736 | tf_op jit(solution)/shard_map/all_gather | solution.py:254
  90.1 7.5 collective-permute-done.6
  116.2 5.8 copy.51
  122.0 6.4 reshape.291
  128.3 6.4 dot_general.122
  134.8 16.4 %fusion.51 = f32[64,64,576]{2,0,1:T(8,128)} fusion(f32[64,576,32]{1,0,2:T(8,128)} %dot_general.122), kind=kOutput, calls=%fused_computation.95 | convolution fusion | flops 905998336 | bytes 14155776 | tf_op jit(solution)/shard_map/dot_general | solution.py:65
  151.2 20.2 %multiply_add_fusion.1 = (f32[64,64,576]{2,0,1:T(8,128)}, f32[64,64,576]{2,0,1:T(8,128)S(1)}) fusion(f32[64,64,576]{2,0,1:T(8,128)} %fusion.51, f32[64,64]{0,1:T(8,128)S(1)} %copy-done.44, f32[64,64]{0,1:T(8,128)S(1)} %copy-done.46, f32[64,576,32]{1,0,2:T(8,128)} %dot_general.122), kind=kOutput, calls=%fused_computation.23 | convolution fusion | flops 922513408 | bytes 33062912 | tf_op jit(solution)/shard_map/dot_general | solution.py:65
  171.4 21.2 %fusion.10 = f32[64,576,64]{1,2,0:T(8,128)} fusion(f32[64,64,576]{2,0,1:T(8,128)S(1)} %get-tuple-element.74), kind=kOutput, calls=%fused_computation.24 | convolution fusion | flops 1811996672 | bytes 18874368 | tf_op jit(solution)/shard_map/jn,knc->kjc/dot_general | solution.py:71
  192.6 21.2 %fusion.12 = f32[64,576,64]{1,2,0:T(8,128)} fusion(f32[64,64,576]{2,0,1:T(8,128)S(1)} %get-tuple-element.74), kind=kOutput, calls=%fused_computation.26 | convolution fusion | flops 1811996672 | bytes 18874368 | tf_op jit(solution)/shard_map/jn,knc->kjc/dot_general | solution.py:71
  213.8 23.6 %subtract_bitcast_fusion.2 = f32[64,64,576]{2,1,0:T(8,128)} fusion(f32[64,576,64]{1,2,0:T(8,128)} %fusion.10, f32[64,64,576]{2,0,1:T(8,128)} %get-tuple-element.73), kind=kOutput, calls=%fused_computation.20 | convolution fusion | flops 1814355968 | bytes 28311552 | tf_op jit(solution)/shard_map/jn,knc->kjc/dot_general | solution.py:71
  237.3 22.4 %add_bitcast_fusion.2 = f32[64,64,576]{2,1,0:T(8,128)S(1)} fusion(f32[64,576,64]{1,2,0:T(8,128)} %fusion.12, f32[64,64,576]{2,0,1:T(8,128)} %get-tuple-element.73), kind=kOutput, calls=%fused_computation.21 | convolution fusion | flops 1814355968 | bytes 28311552 | tf_op jit(solution)/shard_map/jn,knc->kjc/dot_general | solution.py:71
  268.5 10.7 tile.17
  285.8 11.1 tile.19
  296.9 9.5 multiply_subtract_fusion.5
  306.5 7.9 fusion.97
  314.3 7.8 fusion.109
  322.1 7.9 fusion.99
  330.0 14.9 %multiply_add_fusion.4 = (f32[64,384,64]{1,2,0:T(8,128)}, f32[64,384,64]{1,2,0:T(8,128)}) fusion(f32[64,64]{1,0:T(8,128)S(1)} %copy-done.37, f32[64,64]{1,0:T(8,128)S(1)} %copy-done.39, f32[64,384,64]{1,2,0:T(8,128)} %fusion.97, f32[64,384,64]{1,2,0:T(8,128)} %fusion.109, f32[64,384,64]{1,2,0:T(8,128)} %fusion.99, f32[64,64,384]{2,1,0:T(8,128)S(1)} %get-tuple-element.70), kind=kOutput, calls=%fused_computation.90 | convolution fusion | flops 1220599808 | bytes 37781504 | tf_op jit(solution)/shard_map/jn,knc->kjc/dot_general | solution.py:71
  344.9 6.5 copy.80
  358.5 5.5 fusion.1
  367.3 4.9 fusion.294
  385.6 65.8 %all-reduce.23.cloned.1.call-done = bf16[2048,768]{1,0:T(8,128)(2,1)} async-done(((bf16[2048,768]{1,0:T(8,128)(2,1)}), bf16[2048,768]{1,0:T(8,128)(2,1)}) %all-reduce.23.cloned.1.call-update) | async-done | bytes 3145744 | tf_op jit(solution)/shard_map/psum | solution.py:228
  462.1 19.1 %fusion.287 = (bf16[768]{0:T(1024)(128)(2,1)}, bf16[2048,768]{1,0:T(8,128)(2,1)S(1)}, f32[2048,768]{1,0:T(8,128)}) fusion(f32[2048,768]{1,0:T(8,128)S(1)} %fusion.282, f32[768]{0:T(1024)S(1)} %copy-done.85, bf16[2048,768]{1,0:T(8,128)(2,1)S(1)} %copy-done.24, bf16[768,768]{1,0:T(8,128)(2,1)S(1)} %copy-done), kind=kOutput, calls=%fused_computation.391 | convolution fusion | flops 2532310272 | bytes 20058624 | tf_op jit(solution)/shard_map/dot_general | solution.py:59
  486.9 5.5 multiply_convert_fusion
  494.1 4.5 convolution_convert_fusion.1
  498.6 57.0 %all-reduce.25.cloned.1.call-done = bf16[2048,768]{1,0:T(8,128)(2,1)} async-done(((bf16[2048,768]{1,0:T(8,128)(2,1)}), bf16[2048,768]{1,0:T(8,128)(2,1)}) %all-reduce.25.cloned.1.call-update) | async-done | bytes 3145744 | tf_op jit(solution)/shard_map/psum | solution.py:246
  555.6 5.7 fusion.40
  562.1 5.2 fusion.41
  571.7 5.6 multiply_reduce_fusion.4
  582.3 9.1 copy.62
  591.5 9.0 reshape.294
  600.4 8.9 dot_general.142
  609.3 25.4 %fusion.30 = f32[64,64,960]{2,0,1:T(8,128)} fusion(f32[64,960,32]{1,0,2:T(8,128)} %dot_general.142), kind=kOutput, calls=%fused_computation.46 | convolution fusion | flops 1509978112 | bytes 23592960 | tf_op jit(solution)/shard_map/dot_general | solution.py:65
  634.8 26.6 %multiply_add_fusion = (f32[64,64,960]{2,0,1:T(8,128)}, f32[64,64,960]{2,0,1:T(8,128)}) fusion(f32[64,64,960]{2,0,1:T(8,128)} %fusion.30, f32[64,64]{0,1:T(8,128)S(1)} %copy-done.45, f32[64,64]{0,1:T(8,128)S(1)} %copy-done.47, f32[64,960,32]{1,0,2:T(8,128)S(1)} %copy-done.10), kind=kOutput, calls=%fused_computation.7 | convolution fusion | flops 1537503232 | bytes 55083008 | tf_op jit(solution)/shard_map/dot_general | solution.py:65
  661.4 36.1 %fusion.2 = f32[64,960,64]{1,2,0:T(8,128)} fusion(f32[64,64,960]{2,0,1:T(8,128)} %get-tuple-element.66), kind=kOutput, calls=%fused_computation.8 | convolution fusion | flops 3019956224 | bytes 31457280 | tf_op jit(solution)/shard_map/jn,knc->kjc/dot_general | solution.py:71
  697.5 36.5 %fusion.4 = f32[64,960,64]{1,2,0:T(8,128)} fusion(f32[64,64,960]{2,0,1:T(8,128)} %get-tuple-element.66), kind=kOutput, calls=%fused_computation.10 | convolution fusion | flops 3019956224 | bytes 31457280 | tf_op jit(solution)/shard_map/jn,knc->kjc/dot_general | solution.py:71
  734.0 32.7 %subtract_bitcast_fusion = f32[64,64,960]{2,1,0:T(8,128)} fusion(f32[64,960,64]{1,2,0:T(8,128)} %fusion.2, f32[64,64,960]{2,0,1:T(8,128)} %get-tuple-element.65), kind=kOutput, calls=%fused_computation.4 | convolution fusion | flops 3023888384 | bytes 47185920 | tf_op jit(solution)/shard_map/jn,knc->kjc/dot_general | solution.py:71
  766.6 32.6 %add_bitcast_fusion = f32[64,64,960]{2,1,0:T(8,128)} fusion(f32[64,960,64]{1,2,0:T(8,128)} %fusion.4, f32[64,64,960]{2,0,1:T(8,128)} %get-tuple-element.65), kind=kOutput, calls=%fused_computation.5 | convolution fusion | flops 3023888384 | bytes 47185920 | tf_op jit(solution)/shard_map/jn,knc->kjc/dot_general | solution.py:71
  805.9 10.7 tile.41
  823.3 10.8 tile.43
  834.1 23.9 %multiply_add_fusion.3 = (f32[64,64,384]{2,1,0:T(8,128)}, f32[64,64,384]{2,1,0:T(8,128)}, f32[64,64,384]{2,1,0:T(8,128)}, f32[64,64,384]{2,1,0:T(8,128)}) fusion(f32[64,64,384]{2,1,0:T(8,128)} %tile.43, f32[64,64,384]{2,1,0:T(8,128)} %tile.41, f32[64,64,960]{2,1,0:T(8,128)} %subtract_bitcast_fusion, f32[64,64,960]{2,1,0:T(8,128)} %add_bitcast_fusion), kind=kLoop, calls=%fused_computation.71 | loop fusion | flops 18874368 | bytes 62914560 | tf_op jit(solution)/shard_map/add | solution.py:168
  857.9 4.7 slice_add_fusion
  863.2 12.4 fusion.26
  875.6 12.7 fusion.27
  888.2 4.6 slice_add_fusion.1
  894.8 12.5 fusion.28
  907.3 28.0 %add_bitcast_fusion.1 = (f32[64,64,576]{2,1,0:T(8,128)}, f32[64,64,576]{2,1,0:T(8,128)}) fusion(f32[64,64]{1,0:T(8,128)S(1)} %copy-done.38, f32[64,64]{1,0:T(8,128)S(1)} %copy-done.40, f32[64,576,64]{1,2,0:T(8,128)} %fusion.26, f32[64,576,64]{1,2,0:T(8,128)} %fusion.28, f32[64,576,64]{1,2,0:T(8,128)} %fusion.27, f32[64,64,192]{2,1,0:T(8,128)} %copy-done.16, ...), kind=kOutput, calls=%fused_computation.18 | convolution fusion | flops 1833230336 | bytes 56655872 | tf_op jit(solution)/shard_map/jn,knc->kjc/dot_general | solution.py:71
  935.3 11.9 reshape.296
  947.2 11.9 reshape.295
  959.1 7.7 fusion.164
  966.8 6.7 fusion
  973.5 6.6 div.75
  980.1 6.6 fusion.293
  1004.8 5.3 multiply_reduce_fusion.3
  1018.9 6.7 convolution_convert_fusion.3
  1025.6 7.5 convolution_convert_fusion.4
  1043.4 14.3 %reduce-scatter.2.cloned.1.call-done = bf16[256,192]{0,1:T(8,128)(2,1)} async-done(((bf16[2048,192]{0,1:T(8,128)(2,1)}), bf16[256,192]{0,1:T(8,128)(2,1)}) %reduce-scatter.2.cloned.1.call-update) | async-done | bytes 98320 | tf_op jit(solution)/shard_map/reduce_scatter | solution.py:271
  1059.3 120.2 %all-reduce.29.cloned.1.call-done = (bf16[2048,768]{1,0:T(8,128)(2,1)}, bf16[2048,768]{1,0:T(8,128)(2,1)}) async-done(((bf16[2048,768]{1,0:T(8,128)(2,1)}, bf16[2048,768]{1,0:T(8,128)(2,1)}), (bf16[2048,768]{1,0:T(8,128)(2,1)}, bf16[2048,768]{1,0:T(8,128)(2,1)})) %all-reduce.29.cloned.1.call-update) | async-done | bytes 6291472 | tf_op jit(solution)/shard_map/psum | solution.py:236
  1186.1 5.1 fusion.42
  1191.2 39.5 %all-reduce.15 = (bf16[768]{0:T(1024)(128)(2,1)S(1)}, bf16[768]{0:T(1024)(128)(2,1)S(1)}, bf16[3,192]{1,0:T(4,128)(2,1)S(1)}, bf16[3,3,192]{2,1,0:T(4,128)(2,1)S...) all-reduce(bf16[768]{0:T(1024)(128)(2,1)S(1)} %get-tuple-element.20, ...), channel_id=1, replica_groups=mesh['dp'=8,'mp'=4] {'dp'}, use_global_device_ids=true, to_apply=%region_13.14 | all-reduce | flops 8064 | bytes 32256 | tf_op jit(solution)/shard_map/psum | solution.py:291
  1237.2 12.7 add_add_fusion.2
  1249.9 76.8 %all-reduce.27.cloned.1.call-done = (bf16[768,3,192]{0,2,1:T(8,128)(2,1)}, bf16[192,768]{1,0:T(8,128)(2,1)}, bf16[768,768]{1,0:T(8,128)(2,1)}, bf16[768,768]{1,0:T(8,128)(2,1)}) async-done(((bf16[768,3,192]{0,2,1:T(8,128)(2,1)}, bf16[192,768]{1,0:T(8,128)(2,1)}, bf16[768,768]{1,0:T(8,128)(2,1)}, bf16[768,768]{1,0:T(8,128)(2,1)}), (bf16[768,3,192]{0,2,1:T(8,128)(2,1)}, bf16[192,768]{1,0:T(8,128)(2,1)}, ...) | async-done | bytes 3538960 | tf_op jit(solution)/shard_map/psum | solution.py:293
  (341 shorter events, 198.1 us)
Async XLA Ops:
  7.2 454.8 %copy-start = (bf16[768,768]{1,0:T(8,128)(2,1)S(1)}, bf16[768,768]{1,0:T(8,128)(2,1)}, u32[]{:S(2)}) copy-start(bf16[768,768]{1,0:T(8,128)(2,1)} %param.35) | copy-start | bytes 3538948
  7.2 12.1 copy-start.81
  7.2 12.1 copy-start.73
  7.2 12.1 copy-start.96
  7.2 12.1 copy-start.92
  7.3 444.1 %all-reduce.23.cloned.1.call-start = ((), (), s32[]{:S(2)}) async-start(), calls=%async_computation.1 | async-start | bytes 6291456 | tf_op jit(solution)/shard_map/psum | solution.py:228
  7.3 18.2 %collective-permute-start = (bf16[256,192]{0,1:T(8,128)(2,1)}, bf16[256,192]{0,1:T(8,128)(2,1)S(1)}, u32[]{:S(2)}, u32[]{:S(2)}) collective-permute-start(bf16[256,192]{0,1:T(8,128)(2,1)} %param.26), channel_id=1, source_target_pairs={{0,4},{4,8},{8,12},{12,16},{16,20},{20,24},{24,28},{28,0},{1,5},{5... | collective-permute-start | bytes 294920 | tf_op jit(solution)/shard_map/ppermute | solution.py:219
  12.3 9.4 copy-start.67
  13.0 8.8 copy-start.69
  13.0 564.3 %copy-start.50 = (f32[2048]{0:T(1024)}, f32[2048]{0:T(1024)S(1)}, u32[]{:S(2)}) copy-start(f32[2048]{0:T(1024)S(1)} %get-tuple-element.96) | copy-start | bytes 24580
  25.5 16.7 %copy-start.41 = (bf16[256,192]{0,1:T(8,128)(2,1)}, bf16[256,192]{0,1:T(8,128)(2,1)S(1)}, u32[]{:S(2)}) copy-start(bf16[256,192]{0,1:T(8,128)(2,1)S(1)} %collective-permute-done) | copy-start | bytes 294916
  25.5 7.4 collective-permute-start.1
  32.9 14.8 %copy-start.42 = (bf16[256,192]{0,1:T(8,128)(2,1)}, bf16[256,192]{0,1:T(8,128)(2,1)S(1)}, u32[]{:S(2)}) copy-start(bf16[256,192]{0,1:T(8,128)(2,1)S(1)} %collective-permute-done.1) | copy-start | bytes 294916
  32.9 7.3 collective-permute-start.2
  33.6 545.0 %copy-start.52 = (f32[2048]{0:T(1024)}, f32[2048]{0:T(1024)S(1)}, u32[]{:S(2)}) copy-start(f32[2048]{0:T(1024)S(1)} %fusion.178) | copy-start | bytes 24580
  40.2 7.5 collective-permute-start.3
  47.7 34.3 %collective-permute-start.4 = (bf16[256,192]{0,1:T(8,128)(2,1)}, bf16[256,192]{0,1:T(8,128)(2,1)}, u32[]{:S(2)}, u32[]{:S(2)}) collective-permute-start(bf16[256,192]{0,1:T(8,128)(2,1)} %collective-permute-done.3), channel_id=1, source_target_pairs={{0,4},{4,8},{8,12},{12,16},{16,20},{20,24},{24,28},{28,0},{1,5},{5... | collective-permute-start | bytes 294920 | tf_op jit(solution)/shard_map/ppermute | solution.py:219
  80.7 35.5 %copy-start.28 = (bf16[2048,192]{0,1:T(8,128)(2,1)}, bf16[2048,192]{0,1:T(8,128)(2,1)S(1)}, u32[]{:S(2)}) copy-start(bf16[2048,192]{0,1:T(8,128)(2,1)S(1)} %all_gather.3) | copy-start | bytes 2359300
  82.0 7.6 collective-permute-start.5
  87.4 26.3 %copy-start.31 = (f32[2048,192]{0,1:T(8,128)S(1)}, f32[2048,192]{0,1:T(8,128)}, u32[]{:S(2)}) copy-start(f32[2048,192]{0,1:T(8,128)} %get-tuple-element.57) | copy-start | bytes 4718596
  87.4 26.3 %copy-start.32 = (f32[2048,192]{0,1:T(8,128)S(1)}, f32[2048,192]{0,1:T(8,128)}, u32[]{:S(2)}) copy-start(f32[2048,192]{0,1:T(8,128)} %get-tuple-element.55) | copy-start | bytes 4718596
  89.6 8.0 collective-permute-start.6
  90.1 22.6 %copy-start.61 = (f32[2048]{0:T(1024)}, f32[2048]{0:T(1024)S(1)}, u32[]{:S(2)}) copy-start(f32[2048]{0:T(1024)S(1)} %iota_convert_fusion) | copy-start | bytes 24580
  134.7 16.5 %copy-start.44 = (f32[64,64]{0,1:T(8,128)S(1)}, f32[64,64]{0,1:T(8,128)}, u32[]{:S(2)}) copy-start(f32[64,64]{0,1:T(8,128)} %copy.55) | copy-start | bytes 49156
  134.7 16.5 %copy-start.46 = (f32[64,64]{0,1:T(8,128)S(1)}, f32[64,64]{0,1:T(8,128)}, u32[]{:S(2)}) copy-start(f32[64,64]{0,1:T(8,128)} %copy.53) | copy-start | bytes 49156
  322.1 7.9 copy-start.37
  322.1 7.9 copy-start.39
  367.3 10.4 copy-start.87
  374.9 7.9 copy-start.36
  381.9 69.5 %copy-start.56 = (f32[768]{0:T(1024)S(1)}, f32[768]{0:T(1024)}, u32[]{:S(2)}) copy-start(f32[768]{0:T(1024)} %param.30) | copy-start | bytes 9220
  385.6 72.6 %copy-start.71 = (f32[768]{0:T(1024)S(1)}, f32[768]{0:T(1024)}, u32[]{:S(2)}) copy-start(f32[768]{0:T(1024)} %param.31) | copy-start | bytes 9220
  385.6 72.5 %copy-start.94 = (f32[768]{0:T(1024)S(1)}, f32[768]{0:T(1024)}, u32[]{:S(2)}) copy-start(f32[768]{0:T(1024)} %param.32) | copy-start | bytes 9220
  385.6 170.0 %all-reduce.25.cloned.1.call-start = ((), (), s32[]{:S(2)}) async-start(), calls=%async_computation.2 | async-start | bytes 6291456 | tf_op jit(solution)/shard_map/psum | solution.py:246
  456.1 111.2 %copy-start.54 = (f32[2048]{0:T(1024)}, f32[2048]{0:T(1024)S(1)}, u32[]{:S(2)}) copy-start(f32[2048]{0:T(1024)S(1)} %broadcast_multiply_fusion.4) | copy-start | bytes 24580
  458.1 109.2 %copy-start.63 = (f32[2048]{0:T(1024)}, f32[2048]{0:T(1024)S(1)}, u32[]{:S(2)}) copy-start(f32[2048]{0:T(1024)S(1)} %fusion.180) | copy-start | bytes 24580
  462.1 19.1 %copy-start.30 = (f32[2048,768]{1,0:T(8,128)}, f32[2048,768]{1,0:T(8,128)S(1)}, u32[]{:S(2)}) copy-start(f32[2048,768]{1,0:T(8,128)S(1)} %fusion.282) | copy-start | bytes 18874372
  486.9 570.9 %reduce-scatter.2.cloned.1.call-start = ((), (), s32[]{:S(2)}) async-start(), calls=%async_computation.3 | async-start | bytes 884736 | tf_op jit(solution)/shard_map/reduce_scatter | solution.py:271
  609.3 25.4 %copy-start.10 = (f32[64,960,32]{1,0,2:T(8,128)S(1)}, f32[64,960,32]{1,0,2:T(8,128)}, u32[]{:S(2)}) copy-start(f32[64,960,32]{1,0,2:T(8,128)} %dot_general.142) | copy-start | bytes 23592964
  609.3 25.4 %copy-start.45 = (f32[64,64]{0,1:T(8,128)S(1)}, f32[64,64]{0,1:T(8,128)}, u32[]{:S(2)}) copy-start(f32[64,64]{0,1:T(8,128)} %copy.55) | copy-start | bytes 49156
  609.3 25.4 %copy-start.47 = (f32[64,64]{0,1:T(8,128)S(1)}, f32[64,64]{0,1:T(8,128)}, u32[]{:S(2)}) copy-start(f32[64,64]{0,1:T(8,128)} %copy.53) | copy-start | bytes 49156
  863.2 31.6 %slice-start.6 = ((s8[6291456]{0:T(1024)(128)(4,1)}), s8[4194304]{0:T(1024)(128)(4,1)S(1)}, s32[]{:S(2)}) async-start(s8[6291456]{0:T(1024)(128)(4,1)} %bitcast.171), calls=%async_computation.12 | async-start | bytes 8388608
  875.6 19.2 %slice-start.7 = ((s8[6291456]{0:T(1024)(128)(4,1)}), s8[2097152]{0:T(1024)(128)(4,1)S(1)}, s32[]{:S(2)}) async-start(s8[6291456]{0:T(1024)(128)(4,1)} %bitcast.171), calls=%async_computation.13 | async-start | bytes 4194304
  894.8 12.5 copy-start.38
  894.8 12.5 copy-start.40
  959.1 7.7 copy-start.17
  980.1 9.5 copy-start.22
  992.4 7.5 copy-start.20
  992.4 7.5 copy-start.51
  992.4 7.5 copy-start.53
  992.4 7.5 copy-start.88
  994.3 185.2 %all-reduce.29.cloned.1.call-start = ((), (), s32[]{:S(2)}) async-start(), calls=%async_computation.5 | async-start | bytes 12582912 | tf_op jit(solution)/shard_map/psum | solution.py:236
  997.1 7.7 slice-start
  1018.6 308.2 %all-reduce.27.cloned.1.call-start = ((), (), s32[]{:S(2)}) async-start(), calls=%async_computation.4 | async-start | bytes 7077888 | tf_op jit(solution)/shard_map/psum | solution.py:293
  1018.8 14.3 %slice-start.2 = ((s8[6291456]{0:T(1024)(128)(4,1)}), s8[4194304]{0:T(1024)(128)(4,1)S(1)}, s32[]{:S(2)}) async-start(s8[6291456]{0:T(1024)(128)(4,1)} %bitcast.169), calls=%async_computation.8 | async-start | bytes 8388608
  1025.6 7.6 slice-start.3
  1025.6 7.5 copy-start.27
  1041.0 145.1 %copy-start.66 = (f32[2048]{0:T(1024)S(1)}, f32[2048]{0:T(1024)}, u32[]{:S(2)}) copy-start(f32[2048]{0:T(1024)} %copy-done.65) | copy-start | bytes 24580
  1181.9 9.3 copy-start.83
  1181.9 9.3 copy-start.84
  1181.9 9.3 copy-start.89
  1181.9 9.3 copy-start.90
  1181.9 55.3 %copy-start.60 = (f32[2048]{0:T(1024)S(1)}, f32[2048]{0:T(1024)}, u32[]{:S(2)}) copy-start(f32[2048]{0:T(1024)} %copy-done.58) | copy-start | bytes 24580
  1181.9 55.3 %copy-start.86 = (f32[768]{0:T(1024)S(1)}, f32[768]{0:T(1024)}, u32[]{:S(2)}) copy-start(f32[768]{0:T(1024)} %param.36) | copy-start | bytes 9220
  1237.2 98.4 %copy-start.1 = (bf16[768,768]{1,0:T(8,128)(2,1)S(1)}, bf16[768,768]{1,0:T(8,128)(2,1)}, u32[]{:S(2)}) copy-start(bf16[768,768]{1,0:T(8,128)(2,1)} %param.35) | copy-start | bytes 3538948
  (57 other events, 236.6 us)
Sparse Core Ops, SparseCore 0:
  385.7 65.6 all-reduce.22
  487.0 68.5 all-reduce.24
  994.4 63.2 reduce-scatter.1
  1060.7 118.7 all-reduce.28
  1185.5 141.1 all-reduce.26
